TPU v7x, 512 devices: a whole 4x8x8 slice. The times are simulated.
512 devices in a mesh: gx: 16 (over y, core), gy: 32 (over z, x).
Axes of the slice: x: 4, y: 8, z: 8, core: 2. Of those that a mesh axis runs over, the one named last changes fastest.
Arguments:
- inputs: bfloat16 [256, 4, 2304], P('gy', None, 'gx'), may hold values from -8 to 8
- cache_pool: bfloat16 [2, 64, 4096, 1024], P(None, 'gx', 'gy'), may hold values from -6 to 6
- lengths: int32 [32], P('gy'), may hold values from 1 to 32768, as said below
- block_table: int32 [32, 33], P('gy'), may hold values from -1 to 63, as said below
- parents: int32 [3, 256], P(None, 'gy'), may hold values from 0 to 7
- norm_gains: float32 [4, 2304], P(None, 'gx'), may hold values from -0.5 to 1
- w_query: bfloat16 [2304, 2048], P('gx', 'gy'), may hold values from -0.125 to 0.125
- w_key: bfloat16 [2304, 1024], P('gx', 'gy'), may hold values from -0.125 to 0.125
- w_value: bfloat16 [2304, 1024], P('gx', 'gy'), may hold values from -0.125 to 0.125
- w_out: bfloat16 [2048, 2304], P('gy', 'gx'), may hold values from -1 to 1
- w_gate: bfloat16 [2304, 9216], P('gx', 'gy'), may hold values from -0.125 to 0.125
- w_up: bfloat16 [2304, 9216], P('gx', 'gy'), may hold values from -0.125 to 0.125
- w_down: bfloat16 [9216, 2304], P('gy', 'gx'), may hold values from -1 to 1
Outputs:
- outputs: bfloat16 [256, 4, 2304], P('gy', None, 'gx')
Inputs may be any that keep to these rules, and one draw needn't show every extreme that they name: `lengths`: a group's beams share its prompt length. block_table[g, j] is the slot, numbered over the index of gy that holds group g as gx index times 4 plus the device's slot, of page first(g) + j of the group, for j up to (lengths[g] - 1) // 128 - first(g), and -1 beyond; no slot is named twice; a device holds at most 4 pages, and some device holds 4. Beam b at step s + 1 continues beam parents[s, b] of its own group, numbered within the group.
All inputs are finite; a program needn't handle non-finite values.
Results may differ from a plain program's by a relative error of at most 0.015.
Values may be sent and summed in bfloat16 or wider, within the bound.
A program may use at most 64 MiB of HBM per device.

v0:
```python
import jax
import jax.numpy as jnp
from jax import lax
from jax.sharding import PartitionSpec as P

D = 2304
HEADS = 8
KV_HEADS = 4
HEAD_DIM = 256
WINDOW = 4096
PAGE = 128
BEAM = 8
EPSILON = 1e-06
SOFT_CAP = 50.0
ROPE_BASE = 10000.0


def rotate(values, positions):
    half_width = values.shape[-1] // 2
    inverse_freq = ROPE_BASE ** (
        -jnp.arange(half_width, dtype=jnp.float32) * 2.0 / values.shape[-1]
    )
    angles = positions[..., None].astype(jnp.float32) * inverse_freq
    cosine = jnp.cos(angles)[..., None, :]
    sine_part = jnp.sin(angles)[..., None, :]
    first_half = values[..., :half_width]
    second_half = values[..., half_width:]
    return jnp.concatenate(
        [
            first_half * cosine - second_half * sine_part,
            second_half * cosine + first_half * sine_part,
        ],
        axis=-1,
    )


def ancestry(parents, beam_count, group_size, steps_count):
    beam_ids = jnp.arange(beam_count, dtype=jnp.int32)
    group_base = beam_ids // group_size * group_size
    table_rows = []
    for moment in range(steps_count):
        current = beam_ids
        chain_list = [beam_ids] * steps_count
        for earlier in range(moment, 0, -1):
            current = group_base + jnp.take(parents[earlier - 1], current)
            chain_list[earlier - 1] = current
        table_rows.append(jnp.stack(chain_list))
    return jnp.stack(table_rows)


def tail_terms(grouped, key_steps, value_steps, ancestors):
    steps_count = grouped.shape[1]
    step_ids = jnp.arange(steps_count, dtype=jnp.int32)
    tail_keys = key_steps[ancestors, step_ids[None, :, None]]
    tail_values = value_steps[ancestors, step_ids[None, :, None]]
    scores = jnp.einsum(
        "bskgd,sjbkd->bskgj", grouped, tail_keys, preferred_element_type=jnp.float32
    )
    allowed = step_ids[None, :] <= step_ids[:, None]
    weights = jnp.where(
        allowed[None, :, None, None, :], jnp.exp(SOFT_CAP * jnp.tanh(scores / SOFT_CAP)), 0.0
    )
    numerator = jnp.einsum(
        "bskgj,sjbkd->bskgd",
        weights.astype(jnp.bfloat16),
        tail_values,
        preferred_element_type=jnp.float32,
    )
    return (numerator, jnp.sum(weights, axis=-1))


def body(
    inputs,
    cache_pool,
    lengths,
    block_table,
    parents,
    norm_gains,
    w_query,
    w_key,
    w_value,
    w_out,
    w_gate,
    w_up,
    w_down,
):
    col_beams, steps_count, width_part = inputs.shape
    group_count = lengths.shape[0]
    slot_count = cache_pool.shape[1]
    rep_heads = HEADS // KV_HEADS
    x_wide = inputs.astype(jnp.float32)
    gain_rows = 1.0 + norm_gains
    square_sum = lax.psum(jnp.sum(x_wide * x_wide, axis=-1), "gx")
    normed_share = (x_wide * lax.rsqrt(square_sum / D + EPSILON)[..., None] * gain_rows[0]).astype(
        jnp.bfloat16
    )
    normed = lax.all_gather(normed_share, "gy", axis=0, tiled=True)
    all_beams = normed.shape[0]
    flat_rows = normed.reshape(-1, width_part)

    def project(weight):
        return jnp.dot(flat_rows, weight, preferred_element_type=jnp.float32).reshape(
            all_beams, steps_count, weight.shape[1]
        )

    query_sum, key_sum, value_sum = lax.psum(
        (project(w_query), project(w_key), project(w_value)), "gx"
    )
    query_raw, key_raw, value_raw = (
        lax.all_to_all(query_sum, "gy", split_axis=0, concat_axis=2, tiled=True),
        lax.all_to_all(key_sum, "gy", split_axis=0, concat_axis=2, tiled=True),
        lax.all_to_all(value_sum, "gy", split_axis=0, concat_axis=2, tiled=True),
    )
    beam_lengths = jnp.repeat(lengths, BEAM)
    step_ids = jnp.arange(steps_count, dtype=jnp.int32)
    positions = beam_lengths[:, None] + step_ids[None, :]
    queries = (
        rotate(query_raw.reshape(col_beams, steps_count, HEADS, HEAD_DIM), positions)
        * HEAD_DIM ** (-0.5)
    ).astype(jnp.bfloat16)
    key_steps = rotate(
        key_raw.reshape(col_beams, steps_count, KV_HEADS, HEAD_DIM), positions
    ).astype(jnp.bfloat16)
    value_steps = value_raw.reshape(col_beams, steps_count, KV_HEADS, HEAD_DIM).astype(jnp.bfloat16)
    grouped = queries.reshape(col_beams, steps_count, KV_HEADS, rep_heads, HEAD_DIM)
    slot_ids = lax.axis_index("gx") * slot_count + jnp.arange(slot_count, dtype=jnp.int32)
    matches = block_table[:, :, None] == slot_ids[None, None, :]
    owner_mask = jnp.any(matches, axis=1)
    slot_used = jnp.any(owner_mask, axis=0)
    page_number = jnp.sum(
        jnp.where(matches, jnp.arange(block_table.shape[1], dtype=jnp.int32)[None, :, None], 0),
        axis=(0, 1),
    )
    first_page = jnp.maximum(lengths - WINDOW + 1, 0) // PAGE
    slot_first = jnp.sum(jnp.where(owner_mask, first_page[:, None], 0), axis=0)
    slot_length = jnp.sum(jnp.where(owner_mask, lengths[:, None], 0), axis=0)
    key_positions = (slot_first + page_number)[:, None] * PAGE + jnp.arange(PAGE, dtype=jnp.int32)[
        None, :
    ]
    group_queries = grouped.reshape(group_count, BEAM, steps_count, KV_HEADS, rep_heads, HEAD_DIM)
    slot_queries = jnp.einsum(
        "an,abskgd->nbskgd",
        owner_mask.astype(jnp.bfloat16),
        group_queries,
        preferred_element_type=jnp.float32,
    ).astype(jnp.bfloat16)
    page_keys = cache_pool[0].reshape(slot_count, PAGE, KV_HEADS, HEAD_DIM)
    page_values = cache_pool[1].reshape(slot_count, PAGE, KV_HEADS, HEAD_DIM)
    scores = jnp.einsum(
        "nbskgd,ntkd->nbskgt", slot_queries, page_keys, preferred_element_type=jnp.float32
    )
    lower_bound = slot_length[:, None] + step_ids[None, :] - WINDOW + 1
    visible = (
        slot_used[:, None, None]
        & (key_positions[:, None, :] < slot_length[:, None, None])
        & (key_positions[:, None, :] >= lower_bound[:, :, None])
    )
    weights = jnp.where(
        visible[:, None, :, None, None, :], jnp.exp(SOFT_CAP * jnp.tanh(scores / SOFT_CAP)), 0.0
    )
    page_den = jnp.sum(weights, axis=-1)
    page_num = jnp.einsum(
        "nbskgt,ntkd->nbskgd",
        weights.astype(jnp.bfloat16),
        page_values,
        preferred_element_type=jnp.float32,
    )
    owner_wide = owner_mask.astype(jnp.float32)
    group_num = jnp.sum(owner_wide[:, :, None, None, None, None, None] * page_num[None], axis=1)
    group_den = jnp.sum(owner_wide[:, :, None, None, None, None] * page_den[None], axis=1)
    total_num, total_den = lax.psum((group_num, group_den), "gx")
    ancestors = ancestry(parents, col_beams, BEAM, steps_count)
    tail_num, tail_den = tail_terms(grouped, key_steps, value_steps, ancestors)
    numerator = total_num.reshape(col_beams, steps_count, KV_HEADS, rep_heads, HEAD_DIM) + tail_num
    denominator = total_den.reshape(col_beams, steps_count, KV_HEADS, rep_heads) + tail_den
    attended = (
        (numerator / denominator[..., None])
        .astype(jnp.bfloat16)
        .reshape(col_beams, steps_count, HEADS * HEAD_DIM)
    )
    head_rows = lax.all_to_all(attended, "gy", split_axis=2, concat_axis=0, tiled=True)
    head_width = head_rows.shape[2]
    attn_part = jnp.dot(
        head_rows.reshape(-1, head_width), w_out, preferred_element_type=jnp.float32
    ).reshape(all_beams, steps_count, width_part)
    attn_full = lax.psum(attn_part, "gy")
    residual = lax.all_gather(inputs, "gy", axis=0, tiled=True).astype(jnp.float32)
    attn_square = lax.psum(jnp.sum(attn_full * attn_full, axis=-1), "gx")
    mixed_full = (
        residual + attn_full * lax.rsqrt(attn_square / D + EPSILON)[..., None] * gain_rows[1]
    )
    mixed_square = lax.psum(jnp.sum(mixed_full * mixed_full, axis=-1), "gx")
    ff_input = (
        mixed_full * lax.rsqrt(mixed_square / D + EPSILON)[..., None] * gain_rows[2]
    ).astype(jnp.bfloat16)
    mixed_rows = lax.dynamic_slice_in_dim(
        mixed_full, lax.axis_index("gy") * col_beams, col_beams, 0
    )
    gate_width = w_gate.shape[1]
    matrix_rows = ff_input.reshape(-1, width_part)
    gate_and_up = jnp.concatenate(
        [
            jnp.dot(matrix_rows, w_gate, preferred_element_type=jnp.float32),
            jnp.dot(matrix_rows, w_up, preferred_element_type=jnp.float32),
        ],
        axis=1,
    )
    activate_gate_and_up = lax.psum_scatter(
        gate_and_up.reshape(ff_input.shape[0], steps_count, 2 * gate_width),
        "gx",
        scatter_dimension=0,
        tiled=True,
    )
    hidden_share = (
        jax.nn.gelu(activate_gate_and_up[..., :gate_width], approximate=True)
        * activate_gate_and_up[..., gate_width:]
    ).astype(jnp.bfloat16)
    hidden_rows = lax.all_gather(hidden_share, "gx", axis=0, tiled=True)
    down_part = jnp.dot(
        hidden_rows.reshape(-1, gate_width), w_down, preferred_element_type=jnp.float32
    ).reshape(hidden_rows.shape[0], steps_count, width_part)
    down_own = lax.psum_scatter(down_part, "gy", scatter_dimension=0, tiled=True)
    out_square = lax.psum(jnp.sum(down_own * down_own, axis=-1), "gx")
    return (
        mixed_rows + down_own * lax.rsqrt(out_square / D + EPSILON)[..., None] * gain_rows[3]
    ).astype(jnp.bfloat16)


def solution(mesh):
    return jax.shard_map(
        body,
        mesh=mesh,
        in_specs=(
            P("gy", None, "gx"),
            P(None, "gx", "gy", None),
            P("gy"),
            P("gy", None),
            P(None, "gy"),
            P(None, "gx"),
            P("gx", "gy"),
            P("gx", "gy"),
            P("gx", "gy"),
            P("gy", "gx"),
            P("gx", "gy"),
            P("gx", "gy"),
            P("gy", "gx"),
        ),
        out_specs=P("gy", None, "gx"),
        check_vma=False,
    )
```

profile of v0, /device:TPU:1, one launch (start us, length us, event | category | flops | bytes accessed | tf_op | source)
XLA Modules:
  0.0 937.1 jit_solution(2836527621570253802)
XLA Ops:
  8.1 29.8 %psum.70 = f32[8,4]{0,1:T(4,128)S(1)} all-reduce(f32[8,4]{0,1:T(4,128)S(1)} %fusion.33), channel_id=1, replica_groups=mesh['gx'=16,'gy'=32] {'gx'}, use_global_device_ids=true, to_apply=%region_3.0 | all-reduce | flops 32 | bytes 256 | tf_op jit(solution)/shard_map/psum | solution.py:93
  38.6 36.1 %all_gather.10 = bf16[256,4,144]{2,0,1:T(8,128)(2,1)S(1)} all-gather(bf16[8,4,144]{2,0,1:T(8,128)(2,1)S(1)} %fusion.35), channel_id=1, replica_groups=mesh['gx'=16,'gy'=32] {'gy'}, dimensions={0}, use_global_device_ids=true | all-gather | bytes 304128 | tf_op jit(solution)/shard_map/all_gather | solution.py:97
  74.7 1.7 fusion.37
  79.1 1.8 fusion.65
  84.6 111.0 %all-reduce.9.cloned.1.call-done = f32[256,4,64]{0,2,1:T(8,128)} async-done(((f32[256,4,64]{0,2,1:T(8,128)}), f32[256,4,64]{0,2,1:T(8,128)}) %all-reduce.9.cloned.1.call-update) | async-done | bytes 262160 | tf_op jit(solution)/shard_map/psum | solution.py:106
  198.0 9.9 %all-to-all-start = ((f32[32,1,2048]{2,1,0:T(1,128)}), f32[32,1,2048]{2,1,0:T(1,128)S(1)}, u32[]{:S(2)}, u32[]{:S(2)}) async-start(f32[32,1,2048]{2,1,0:T(1,128)} %reshape.614), calls=%async_computation | async-start | bytes 524288 | tf_op jit(solution)/shard_map/all_to_all | solution.py:110
  211.6 7.5 all-to-all-done
  221.9 1.7 fusion.67
  225.1 47.4 %all-reduce.16 = (bf16[256,4,32]{0,2,1:T(8,128)(2,1)S(1)}, f32[8,4,4,2]{0,2,3,1:T(4,128)S(1)}) all-reduce(f32[256,4,32]{0,2,1:T(8,128)S(1)} %fusion.42, f32[8,4,4,2]{0,2,3,1:T(4,128)S(1)} %copy.223), channel_id=1, replica_groups=mesh['gx'=16,'gy'=32] {'gx'}, use_global_device_ids=true, to_apply=%region_8.10 | all-reduce | flops 33024 | bytes 198656 | tf_op jit(solution)/shard_map/psum | solution.py:106
  273.5 3.8 all-to-all-start.2
  278.1 120.2 %all-reduce.15.cloned.1.call-done = (f32[8,4,4,2,256]{4,3,2,1,0:T(2,128)}, f32[256,4,32]{0,2,1:T(8,128)}) async-done(((f32[8,4,4,2,256]{4,3,2,1,0:T(2,128)}, f32[256,4,32]{0,2,1:T(8,128)}), (f32[8,4,4,2,256]{4,3,2,1,0:T(2,128)}, f32[256,4,32]{0,2,1:T(8,128)})) %all-reduce.15.cloned.1.call-update) | async-done | bytes 393232 | tf_op jit(solution)/shard_map/psum | solution.py:171
  400.4 9.9 %all-to-all-start.1 = ((f32[32,1,1024]{2,1,0:T(1,128)}), f32[32,1,1024]{2,1,0:T(1,128)S(1)}, u32[]{:S(2)}, u32[]{:S(2)}) async-start(f32[32,1,1024]{2,1,0:T(1,128)} %reshape.618), calls=%async_computation.1 | async-start | bytes 262144 | tf_op jit(solution)/shard_map/all_to_all | solution.py:111
  412.2 7.5 all-to-all-done.1
  425.0 2.3 reshape.620
  427.3 12.7 %all_to_all.54 = bf16[32,2,1024]{2,1,0:T(2,128)(2,1)S(1)} all-to-all(bf16[32,2,1024]{2,1,0:T(2,128)(2,1)S(1)} %reshape.620), channel_id=1, replica_groups=mesh['gx'=16,'gy'=32] {'gy'}, dimensions={0} | all-to-all | bytes 262144 | tf_op jit(solution)/shard_map/all_to_all | solution.py:181
  440.0 2.4 reshape.621
  442.5 2.1 copy.252
  446.0 37.6 %all_gather.9 = bf16[256,4,144]{2,1,0:T(4,128)(2,1)S(1)} all-gather(bf16[8,4,144]{2,1,0:T(4,128)(2,1)S(1)} %copy-done.2), channel_id=1, replica_groups=mesh['gx'=16,'gy'=32] {'gy'}, dimensions={0}, use_global_device_ids=true | all-gather | bytes 304128 | tf_op jit(solution)/shard_map/all_gather | solution.py:187
  483.6 115.7 %all-reduce.11.cloned.1.call-done = f32[256,4,144]{2,0,1:T(8,128)} async-done(((f32[256,4,144]{2,0,1:T(8,128)}), f32[256,4,144]{2,0,1:T(8,128)}) %all-reduce.11.cloned.1.call-update) | async-done | bytes 589840 | tf_op jit(solution)/shard_map/psum | solution.py:186
  599.3 1.4 multiply_reduce_fusion.1
  600.8 28.1 %psum.77 = f32[256,4]{0,1:T(4,128)S(1)} all-reduce(f32[256,4]{0,1:T(4,128)S(1)} %multiply_reduce_fusion.1), channel_id=1, replica_groups=mesh['gx'=16,'gy'=32] {'gx'}, use_global_device_ids=true, to_apply=%region_15.17 | all-reduce | flops 1024 | bytes 8192 | tf_op jit(solution)/shard_map/psum | solution.py:188
  628.9 1.6 multiply_reduce_fusion
  630.5 23.6 %psum.78 = f32[256,4]{0,1:T(4,128)S(1)} all-reduce(f32[256,4]{0,1:T(4,128)S(1)} %get-tuple-element.12), channel_id=1, replica_groups=mesh['gx'=16,'gy'=32] {'gx'}, use_global_device_ids=true, to_apply=%region_17.19 | all-reduce | flops 1024 | bytes 8192 | tf_op jit(solution)/shard_map/psum | solution.py:192
  655.9 1.6 pad_maximum_fusion
  657.4 2.1 copy.232
  659.5 1.9 reshape.525
  661.5 3.4 copy.233
  665.0 57.8 %reduce-scatter.2.cloned.1.call-done = f32[16,4,576]{2,0,1:T(8,128)} async-done(((f32[256,4,576]{2,0,1:T(8,128)}), f32[16,4,576]{2,0,1:T(8,128)}) %reduce-scatter.2.cloned.1.call-update) | async-done | bytes 147472 | tf_op jit(solution)/shard_map/reduce_scatter | solution.py:208
  723.8 19.0 %all_gather.11 = bf16[256,4,288]{2,0,1:T(8,128)(2,1)S(1)} all-gather(bf16[16,4,288]{2,0,1:T(8,128)(2,1)S(1)} %fusion.31), channel_id=1, replica_groups=mesh['gx'=16,'gy'=32] {'gx'}, dimensions={0}, use_global_device_ids=true | all-gather | bytes 626688 | tf_op jit(solution)/shard_map/all_gather | solution.py:218
  743.3 1.7 copy.234
  746.9 153.2 %all-reduce.13.cloned.1.call-done = f32[256,4,144]{2,1,0:T(4,128)} async-done(((f32[256,4,144]{2,1,0:T(4,128)}), f32[256,4,144]{2,1,0:T(4,128)}) %all-reduce.13.cloned.1.call-update) | async-done | bytes 589840
  901.0 28.1 %psum.79 = f32[8,4]{0,1:T(4,128)S(1)} all-reduce(f32[8,4]{0,1:T(4,128)S(1)} %copy.235), channel_id=1, replica_groups=mesh['gx'=16,'gy'=32] {'gx'}, use_global_device_ids=true, to_apply=%region_21.23 | all-reduce | flops 32 | bytes 256 | tf_op jit(solution)/shard_map/psum | solution.py:223
  (128 shorter events, 37.4 us)
Async XLA Ops:
  6.5 648.6 %copy-start = (bf16[144,288]{1,0:T(8,128)(2,1)S(1)}, bf16[144,288]{1,0:T(8,128)(2,1)}, u32[]{:S(2)}) copy-start(bf16[144,288]{1,0:T(8,128)(2,1)} %param.25) | copy-start | bytes 248836
  6.5 189.0 %all-reduce.9.cloned.1.call-start = ((), (), s32[]{:S(2)}) async-start(), calls=%async_computation.5 | async-start | bytes 524288 | tf_op jit(solution)/shard_map/psum | solution.py:106
  79.1 1.8 copy-start.8
  80.9 3.3 copy-start.6
  198.0 21.1 %all-to-all-start = ((f32[32,1,2048]{2,1,0:T(1,128)}), f32[32,1,2048]{2,1,0:T(1,128)S(1)}, u32[]{:S(2)}, u32[]{:S(2)}) async-start(f32[32,1,2048]{2,1,0:T(1,128)} %reshape.614), calls=%async_computation | async-start | bytes 524288 | tf_op jit(solution)/shard_map/all_to_all | solution.py:110
  208.5 2.1 copy-start.7
  273.5 126.9 %all-to-all-start.2 = ((bf16[32,2,512]{2,1,0:T(2,128)(2,1)}), bf16[32,2,512]{2,1,0:T(2,128)(2,1)S(1)}, u32[]{:S(2)}, u32[]{:S(2)}) async-start(bf16[32,2,512]{2,1,0:T(2,128)(2,1)} %reshape.616), calls=%async_computation.2 | async-start | bytes 131072 | tf_op jit(solution)/shard_map/all_to_all | solution.py:112
  277.3 121.0 %all-reduce.15.cloned.1.call-start = ((), (), s32[]{:S(2)}) async-start(), calls=%async_computation.9 | async-start | bytes 786432 | tf_op jit(solution)/shard_map/psum | solution.py:171
  400.4 19.3 %all-to-all-start.1 = ((f32[32,1,1024]{2,1,0:T(1,128)}), f32[32,1,1024]{2,1,0:T(1,128)S(1)}, u32[]{:S(2)}, u32[]{:S(2)}) async-start(f32[32,1,1024]{2,1,0:T(1,128)} %reshape.618), calls=%async_computation.1 | async-start | bytes 262144 | tf_op jit(solution)/shard_map/all_to_all | solution.py:111
  410.3 189.0 %all-reduce.11.cloned.1.call-start = ((), (), s32[]{:S(2)}) async-start(), calls=%async_computation.6 | async-start | bytes 2097152 | tf_op jit(solution)/shard_map/psum | solution.py:186
  421.3 2.0 copy-start.9
  440.0 4.6 copy-start.5
  442.5 3.5 copy-start.2
  445.9 276.8 %reduce-scatter.2.cloned.1.call-start = ((), (), s32[]{:S(2)}) async-start(), calls=%async_computation.7 | async-start | bytes 2785280 | tf_op jit(solution)/shard_map/reduce_scatter | solution.py:208
  630.5 23.8 %copy-start.1 = (f32[256,4,144]{2,0,1:T(8,128)}, f32[256,4,144]{2,0,1:T(8,128)S(1)}, u32[]{:S(2)}) copy-start(f32[256,4,144]{2,0,1:T(8,128)S(1)} %get-tuple-element.13) | copy-start | bytes 1769476
  654.3 1.1 copy-start.3
  664.9 77.9 %copy-start.4 = (bf16[288,144]{0,1:T(8,128)(2,1)S(1)}, bf16[288,144]{0,1:T(8,128)(2,1)}, u32[]{:S(2)}) copy-start(bf16[288,144]{0,1:T(8,128)(2,1)} %param.27) | copy-start | bytes 248836
  664.9 235.2 %all-reduce.13.cloned.1.call-start = ((), (), s32[]{:S(2)}) async-start(), calls=%async_computation.8 | async-start | bytes 2097152
Sparse Core Ops, SparseCore 0:
  76.6 118.8 all-reduce.8
  280.7 117.4 all-reduce.14
  446.0 153.2 all-reduce.10
  665.0 57.6 reduce-scatter.1
  745.1 154.9 all-reduce.12
where the time goes:
time: 938 us; the launch traced here: 937 us
  waiting for transfers between devices  574 us (61%)
  blocking collectives  262 us (28%)
  local copies, waits for them, and re-layouts  38.9 us (4%)
  starting transfers between devices  24 us (3%)
  between operations  15 us (2%)
  other arithmetic  14.8 us (2%)
    unnamed x6, waiting for transfers between devices  154 us
    psum x1, waiting for transfers between devices, body(): total_num, total_den = lax.psum((group_num, group_den), 'gx')  120 us
    psum x1, waiting for transfers between devices, body(): attn_full = lax.psum(attn_part, 'gy')  116 us
    psum x1, waiting for transfers between devices, body(): lax.psum((project(w_query), project(w_key), project(w_value)), 'gx')  111 us
    reduce_scatter x1, waiting for transfers between devices, body(): lax.psum_scatter(gate_and_up.reshape(ff_input.shape[0], steps_count, 2 *...  57.8 us
    psum x1, blocking collectives, body(): lax.psum((project(w_query), project(w_key), project(w_value)), 'gx')  47.4 us
    all_gather x1, blocking collectives, body(): lax.all_gather(inputs, 'gy', axis=0, tiled=True).astype(jnp.float32)  37.6 us
    all_gather x1, blocking collectives, body(): normed = lax.all_gather(normed_share, 'gy', axis=0, tiled=True)  36.1 us
  transfers between devices with their start and end apart: 8, of which 7 were waited for; matrix products, arithmetic and copies ran while one was open for 2% of the time, Pallas kernels for 0%

commit v1 on v0

--- a/solution.py
+++ b/solution.py
@@ -215,7 +215,24 @@
         jax.nn.gelu(activate_gate_and_up[..., :gate_width], approximate=True)
         * activate_gate_and_up[..., gate_width:]
     ).astype(jnp.bfloat16)
-    hidden_rows = lax.all_gather(hidden_share, "gx", axis=0, tiled=True)
+    size, here, rows = (lax.axis_size("gx"), lax.axis_index("gx"), hidden_share.shape[0])
+    upward = [(i, (i + 1) % size) for i in range(size)]
+    downward = [(i, (i - 1) % size) for i in range(size)]
+    out = jnp.zeros(
+        (*hidden_share.shape[:0], size * rows, *hidden_share.shape[0 + 1 :]), hidden_share.dtype
+    )
+    out = lax.dynamic_update_slice_in_dim(out, hidden_share, here * rows, axis=0)
+    from_left = from_right = hidden_share
+    middle = size // 2
+    for step in range(1, middle + 1):
+        from_left = lax.ppermute(from_left, "gx", upward)
+        out = lax.dynamic_update_slice_in_dim(out, from_left, (here - step) % size * rows, axis=0)
+        if step < size - middle:
+            from_right = lax.ppermute(from_right, "gx", downward)
+            out = lax.dynamic_update_slice_in_dim(
+                out, from_right, (here + step) % size * rows, axis=0
+            )
+    hidden_rows = out
     down_part = jnp.dot(
         hidden_rows.reshape(-1, gate_width), w_down, preferred_element_type=jnp.float32
     ).reshape(hidden_rows.shape[0], steps_count, width_part)

time: 938 us -> 1060 us (1.13)
  waiting for transfers between devices: 574 us -> 643 us
  local copies, waits for them, and re-layouts: 38.9 us -> 76 us
  starting transfers between devices: 24 us -> 49 us
  blocking collectives: 262 us -> 243 us
    unnamed x6 -> x7, waiting for transfers between devices: 154 us -> 276 us
    reduce_scatter x1 -> x0, waiting for transfers between devices: 57.8 us -> none  [body(): lax.psum_scatter(gate_and_up.reshape(ff_input.shape[0], steps_count, 2 *...]
    dynamic_update_slice x0 -> x16, local copies, waits for them, and re-layouts: none -> 35.2 us  [the longest x8 16.7 us: body(): lax.dynamic_update_slice_in_dim(out, from_left, (here - step) % size * ro...]
    ppermute x0 -> x15, starting transfers between devices: none -> 24.8 us  [the longest x7 22.6 us: body(): from_right = lax.ppermute(from_right, 'gx', downward)]
    all_gather x1 -> x0, blocking collectives: 19 us -> none  [body(): hidden_rows = lax.all_gather(hidden_share, 'gx', axis=0, tiled=True)]
  transfers between devices with their start and end apart: 8 -> 23, of which waited for: 7 -> 18; matrix products, arithmetic and copies ran while one was open for 2% -> 5% of each run, Pallas kernels for 0% -> 0%
where the time goes in v1:
time: 1060 us; the launch traced here: 1050 us
  waiting for transfers between devices  643 us (61%)
  blocking collectives  243 us (23%)
  local copies, waits for them, and re-layouts  76 us (7%)
  starting transfers between devices  49 us (5%)
  between operations  16.2 us (2%)
  other arithmetic  13.8 us (1%)
    unnamed x7, waiting for transfers between devices  276 us
    psum x1, waiting for transfers between devices, body(): total_num, total_den = lax.psum((group_num, group_den), 'gx')  120 us
    psum x1, waiting for transfers between devices, body(): attn_full = lax.psum(attn_part, 'gy')  116 us
    psum x1, waiting for transfers between devices, body(): lax.psum((project(w_query), project(w_key), project(w_value)), 'gx')  111 us
    psum x1, blocking collectives, body(): lax.psum((project(w_query), project(w_key), project(w_value)), 'gx')  47.3 us
    all_gather x1, blocking collectives, body(): lax.all_gather(inputs, 'gy', axis=0, tiled=True).astype(jnp.float32)  37.7 us
    all_gather x1, blocking collectives, body(): normed = lax.all_gather(normed_share, 'gy', axis=0, tiled=True)  36.1 us
    psum x1, blocking collectives, body(): square_sum = lax.psum(jnp.sum(x_wide * x_wide, axis=-1), 'gx')  29.8 us
  transfers between devices with their start and end apart: 23, of which 18 were waited for; matrix products, arithmetic and copies ran while one was open for 5% of the time, Pallas kernels for 0%

profile of v1, /device:TPU:1, one launch (start us, length us, event | category | flops | bytes accessed | tf_op | source)
XLA Modules:
  0.0 1050.3 jit_solution(2087379168428799380)
XLA Ops:
  8.1 29.8 %psum.70 = f32[8,4]{0,1:T(4,128)S(1)} all-reduce(f32[8,4]{0,1:T(4,128)S(1)} %fusion.33), channel_id=1, replica_groups=mesh['gx'=16,'gy'=32] {'gx'}, use_global_device_ids=true, to_apply=%region_3.0 | all-reduce | flops 32 | bytes 256 | tf_op jit(solution)/shard_map/psum | solution.py:93
  38.6 36.1 %all_gather.7 = bf16[256,4,144]{2,0,1:T(8,128)(2,1)S(1)} all-gather(bf16[8,4,144]{2,0,1:T(8,128)(2,1)S(1)} %fusion.35), channel_id=1, replica_groups=mesh['gx'=16,'gy'=32] {'gy'}, dimensions={0}, use_global_device_ids=true | all-gather | bytes 304128 | tf_op jit(solution)/shard_map/all_gather | solution.py:97
  84.7 110.9 %all-reduce.11.cloned.1.call-done = f32[256,4,64]{0,2,1:T(8,128)} async-done(((f32[256,4,64]{0,2,1:T(8,128)}), f32[256,4,64]{0,2,1:T(8,128)}) %all-reduce.11.cloned.1.call-update) | async-done | bytes 262160 | tf_op jit(solution)/shard_map/psum | solution.py:106
  198.0 9.9 all-to-all-start
  211.6 7.5 all-to-all-done
  225.1 47.3 %all-reduce.20 = (bf16[256,4,32]{0,2,1:T(8,128)(2,1)S(1)}, f32[8,4,4,2]{0,2,3,1:T(4,128)S(1)}) all-reduce(f32[256,4,32]{0,2,1:T(8,128)S(1)} %fusion.42, f32[8,4,4,2]{0,2,3,1:T(4,128)S(1)} %copy.313), channel_id=1, replica_groups=mesh['gx'=16,'gy'=32] {'gx'}, use_global_device_ids=true, to_apply=%region_8.10 | all-reduce | flops 33024 | bytes 198656 | tf_op jit(solution)/shard_map/psum | solution.py:106
  273.5 3.8 all-to-all-start.2
  278.1 120.2 %all-reduce.19.cloned.1.call-done = (f32[8,4,4,2,256]{4,3,2,1,0:T(2,128)}, f32[256,4,32]{0,2,1:T(8,128)}) async-done(((f32[8,4,4,2,256]{4,3,2,1,0:T(2,128)}, f32[256,4,32]{0,2,1:T(8,128)}), (f32[8,4,4,2,256]{4,3,2,1,0:T(2,128)}, f32[256,4,32]{0,2,1:T(8,128)})) %all-reduce.19.cloned.1.call-update) | async-done | bytes 393232 | tf_op jit(solution)/shard_map/psum | solution.py:171
  400.4 9.9 all-to-all-start.1
  412.5 7.2 all-to-all-done.1
  427.3 12.7 %all_to_all.54 = bf16[32,2,1024]{2,1,0:T(2,128)(2,1)S(1)} all-to-all(bf16[32,2,1024]{2,1,0:T(2,128)(2,1)S(1)} %reshape.621), channel_id=1, replica_groups=mesh['gx'=16,'gy'=32] {'gy'}, dimensions={0} | all-to-all | bytes 262144 | tf_op jit(solution)/shard_map/all_to_all | solution.py:181
  440.0 2.4 reshape.622
  446.0 37.7 %all_gather.6 = bf16[256,4,144]{2,1,0:T(4,128)(2,1)S(1)} all-gather(bf16[8,4,144]{2,1,0:T(4,128)(2,1)S(1)} %copy-done.2), channel_id=1, replica_groups=mesh['gx'=16,'gy'=32] {'gy'}, dimensions={0}, use_global_device_ids=true | all-gather | bytes 304128 | tf_op jit(solution)/shard_map/all_gather | solution.py:187
  483.7 115.7 %all-reduce.13.cloned.1.call-done = f32[256,4,144]{2,0,1:T(8,128)} async-done(((f32[256,4,144]{2,0,1:T(8,128)}), f32[256,4,144]{2,0,1:T(8,128)}) %all-reduce.13.cloned.1.call-update) | async-done | bytes 589840 | tf_op jit(solution)/shard_map/psum | solution.py:186
  600.8 28.1 %psum.77 = f32[256,4]{0,1:T(4,128)S(1)} all-reduce(f32[256,4]{0,1:T(4,128)S(1)} %multiply_reduce_fusion.1), channel_id=1, replica_groups=mesh['gx'=16,'gy'=32] {'gx'}, use_global_device_ids=true, to_apply=%region_15.17 | all-reduce | flops 1024 | bytes 8192 | tf_op jit(solution)/shard_map/psum | solution.py:188
  630.5 23.6 %psum.78 = f32[256,4]{0,1:T(4,128)S(1)} all-reduce(f32[256,4]{0,1:T(4,128)S(1)} %get-tuple-element.12), channel_id=1, replica_groups=mesh['gx'=16,'gy'=32] {'gx'}, use_global_device_ids=true, to_apply=%region_17.19 | all-reduce | flops 1024 | bytes 8192 | tf_op jit(solution)/shard_map/psum | solution.py:192
  663.5 116.8 %all-reduce.15.cloned.1.call-done = f32[256,4,576]{2,1,0:T(4,128)} async-done(((f32[256,4,576]{2,1,0:T(4,128)}), f32[256,4,576]{2,1,0:T(4,128)}) %all-reduce.15.cloned.1.call-update) | async-done | bytes 2359312
  785.1 2.4 collective-permute-start.3
  788.6 3.6 collective-permute-start.5
  793.1 3.8 collective-permute-start.7
  797.9 3.8 collective-permute-start.9
  802.6 3.8 collective-permute-start.11
  807.3 3.8 collective-permute-start.13
  812.1 2.6 dynamic_update_slice.48
  816.4 2.4 dynamic_update_slice.50
  821.4 2.4 dynamic_update_slice.52
  826.5 2.4 dynamic_update_slice.54
  831.5 2.4 dynamic_update_slice.56
  836.5 2.4 dynamic_update_slice.58
  841.6 2.7 dynamic_update_slice.60
  854.4 158.6 %all-reduce.17.cloned.1.call-done = f32[256,4,144]{2,1,0:T(4,128)} async-done(((f32[256,4,144]{2,1,0:T(4,128)}), f32[256,4,144]{2,1,0:T(4,128)}) %all-reduce.17.cloned.1.call-update) | async-done | bytes 589840
  1014.0 28.1 %psum.79 = f32[8,4]{0,1:T(4,128)S(1)} all-reduce(f32[8,4]{0,1:T(4,128)S(1)} %copy.342), channel_id=1, replica_groups=mesh['gx'=16,'gy'=32] {'gx'}, use_global_device_ids=true, to_apply=%region_21.23 | all-reduce | flops 32 | bytes 256 | tf_op jit(solution)/shard_map/psum | solution.py:240
  (191 shorter events, 88.8 us)
Async XLA Ops:
  6.5 648.6 %copy-start = (bf16[144,288]{1,0:T(8,128)(2,1)S(1)}, bf16[144,288]{1,0:T(8,128)(2,1)}, u32[]{:S(2)}) copy-start(bf16[144,288]{1,0:T(8,128)(2,1)} %param.25) | copy-start | bytes 248836
  6.5 189.0 %all-reduce.11.cloned.1.call-start = ((), (), s32[]{:S(2)}) async-start(), calls=%async_computation.4 | async-start | bytes 524288 | tf_op jit(solution)/shard_map/psum | solution.py:106
  79.1 1.8 copy-start.8
  81.0 3.3 copy-start.6
  198.0 21.1 %all-to-all-start = ((f32[32,1,2048]{2,1,0:T(1,128)}), f32[32,1,2048]{2,1,0:T(1,128)S(1)}, u32[]{:S(2)}, u32[]{:S(2)}) async-start(f32[32,1,2048]{2,1,0:T(1,128)} %reshape.615), calls=%async_computation | async-start | bytes 524288 | tf_op jit(solution)/shard_map/all_to_all | solution.py:110
  208.5 2.1 copy-start.7
  273.5 126.9 %all-to-all-start.2 = ((bf16[32,2,512]{2,1,0:T(2,128)(2,1)}), bf16[32,2,512]{2,1,0:T(2,128)(2,1)S(1)}, u32[]{:S(2)}, u32[]{:S(2)}) async-start(bf16[32,2,512]{2,1,0:T(2,128)(2,1)} %reshape.617), calls=%async_computation.2 | async-start | bytes 131072 | tf_op jit(solution)/shard_map/all_to_all | solution.py:112
  277.3 121.0 %all-reduce.19.cloned.1.call-start = ((), (), s32[]{:S(2)}) async-start(), calls=%async_computation.8 | async-start | bytes 786432 | tf_op jit(solution)/shard_map/psum | solution.py:171
  400.4 19.3 %all-to-all-start.1 = ((f32[32,1,1024]{2,1,0:T(1,128)}), f32[32,1,1024]{2,1,0:T(1,128)S(1)}, u32[]{:S(2)}, u32[]{:S(2)}) async-start(f32[32,1,1024]{2,1,0:T(1,128)} %reshape.619), calls=%async_computation.1 | async-start | bytes 262144 | tf_op jit(solution)/shard_map/all_to_all | solution.py:111
  410.3 189.0 %all-reduce.13.cloned.1.call-start = ((), (), s32[]{:S(2)}) async-start(), calls=%async_computation.5 | async-start | bytes 2097152 | tf_op jit(solution)/shard_map/psum | solution.py:186
  421.3 2.0 copy-start.9
  440.0 4.6 copy-start.5
  442.5 3.5 copy-start.2
  445.9 334.4 %all-reduce.15.cloned.1.call-start = ((), (), s32[]{:S(2)}) async-start(), calls=%async_computation.6 | async-start | bytes 5242880
  630.5 23.8 %copy-start.1 = (f32[256,4,144]{2,0,1:T(8,128)}, f32[256,4,144]{2,0,1:T(8,128)S(1)}, u32[]{:S(2)}) copy-start(f32[256,4,144]{2,0,1:T(8,128)S(1)} %get-tuple-element.13) | copy-start | bytes 1769476
  661.5 351.5 %all-reduce.17.cloned.1.call-start = ((), (), s32[]{:S(2)}) async-start(), calls=%async_computation.7 | async-start | bytes 2097152
  781.4 2.1 collective-permute-start
  781.6 3.5 collective-permute-start.1
  783.5 4.7 collective-permute-start.2
  785.1 3.5 collective-permute-start.3
  788.2 4.7 collective-permute-start.4
  788.6 4.5 collective-permute-start.5
  793.0 4.7 collective-permute-start.6
  793.1 4.7 collective-permute-start.7
  797.7 4.7 collective-permute-start.8
  797.9 4.7 collective-permute-start.9
  802.4 4.7 collective-permute-start.10
  802.6 4.7 collective-permute-start.11
  807.1 4.7 collective-permute-start.12
  807.3 39.3 %collective-permute-start.13 = (bf16[16,4,288]{2,0,1:T(8,128)(2,1)S(1)}, bf16[16,4,288]{2,0,1:T(8,128)(2,1)S(1)}, u32[]{:S(2)}, u32[]{:S(2)}) collective-permute-start(bf16[16,4,288]{2,0,1:T(8,128)(2,1)S(1)} %collective-permute-done.11), channel_id=1, source_target_pairs={{0,480},{32,0},{64,32},{96,64},{128,96},{160,128},{192,160},{224,1... | collective-permute-start | bytes 110600 | tf_op jit(solution)/shard_map/ppermute | solution.py:231
  811.9 36.0 %collective-permute-start.14 = (bf16[16,4,288]{2,0,1:T(8,128)(2,1)S(1)}, bf16[16,4,288]{2,0,1:T(8,128)(2,1)S(1)}, u32[]{:S(2)}, u32[]{:S(2)}) collective-permute-start(bf16[16,4,288]{2,0,1:T(8,128)(2,1)S(1)} %collective-permute-done.12), channel_id=1, source_target_pairs={{0,32},{32,64},{64,96},{96,128},{128,160},{160,192},{192,224},{224... | collective-permute-start | bytes 110600 | tf_op jit(solution)/shard_map/ppermute | solution.py:228
  839.2 11.1 %copy-start.4 = (bf16[288,144]{0,1:T(8,128)(2,1)S(1)}, bf16[288,144]{0,1:T(8,128)(2,1)}, u32[]{:S(2)}) copy-start(bf16[288,144]{0,1:T(8,128)(2,1)} %param.27) | copy-start | bytes 248836
  (1 other events, 1.1 us)
Sparse Core Ops, SparseCore 0:
  76.6 118.8 all-reduce.10
  280.7 117.5 all-reduce.18
  446.0 153.2 all-reduce.12
  661.6 118.6 all-reduce.14
  852.6 160.3 all-reduce.16
